TPU v7x, 32 devices: a whole 2x2x4 slice. The times are simulated.
32 devices in a mesh: seq: 8 (over y, x, core), mp: 4 (over z).
Axes of the slice: x: 2, y: 2, z: 4, core: 2. Of those that a mesh axis runs over, the one named last changes fastest.
Arguments:
- tokens: bfloat16 [1024, 4096], P('seq', 'mp'), may hold values from -10 to 10
- norm_gain: float32 [4096], replicated, may hold values from 0.1 to 1.9
- w_cand: bfloat16 [4096, 4096], P('seq', 'mp'), may hold values from -0.125 to 0.125
- w_gate: bfloat16 [4096, 4096], P('seq', 'mp'), may hold values from -0.046875 to 0.046875
- rec_gate: float32 [4096], P('mp'), may hold values from -0.75 to 0.75
- rec_cand: float32 [4096], P('mp'), may hold values from -0.6 to 0.6
- bias_gate: float32 [4096], P('mp')
- w_out: bfloat16 [4096, 4096], P('mp'), may hold values from -0.09375 to 0.09375
Outputs:
- output: bfloat16 [1024, 4096], P('seq', 'mp')
All inputs are finite; a program needn't handle non-finite values.
Results may differ from a plain program's by a relative error of at most 0.0048.
Values may be sent and summed in bfloat16 or wider, within the bound.
A program may use at most 64 MiB of HBM per device.

v0:
```python
import jax
import jax.numpy as jnp
from jax import lax
from jax.sharding import PartitionSpec as P

NEWTON = 3


def prefix(value, axis, join, neutral):
    count, mine = (lax.axis_size(axis), lax.axis_index(axis))
    pieces = jax.tree.map(lambda part: lax.all_gather(part, axis), value)
    subtotal = jax.tree.map(
        lambda part, zero: jnp.full_like(part, 0) + jnp.asarray(zero, part.dtype), value, neutral
    )

    def lap(position, subtotal):
        longer = join(subtotal, jax.tree.map(lambda part: part[position], pieces))
        return jax.tree.map(lambda new, old: jnp.where(position < mine, new, old), longer, subtotal)

    return lax.fori_loop(0, count - 1, lap, subtotal)


def compose(earlier, later):
    return (later[0] * earlier[0], later[0] * earlier[1] + later[1])


def cell(previous, cand_pre, gate_pre, rec_gate, rec_cand, bias_gate):
    gate = jax.nn.sigmoid(gate_pre + rec_gate * previous + bias_gate)
    cand = jnp.tanh(cand_pre + rec_cand * previous)
    value = gate * previous + (1.0 - gate) * cand
    slope = (
        gate
        + gate * (1.0 - gate) * rec_gate * (previous - cand)
        + (1.0 - gate) * (1.0 - cand * cand) * rec_cand
    )
    return (value, slope)


def per_device(tokens, norm_gain, w_cand, w_gate, rec_gate, rec_cand, bias_gate, w_out):
    tok_rows = tokens.shape[0]
    channels = w_cand.shape[1]
    whole = lax.all_gather(tokens, "mp", axis=1, tiled=True)
    wide = whole.astype(jnp.float32)
    factor = lax.rsqrt(jnp.mean(wide * wide, axis=1, keepdims=True) + 1e-05)
    normed = (wide * factor * norm_gain).astype(jnp.bfloat16)
    cand_pre = jnp.dot(
        normed,
        lax.all_gather(w_cand, "seq", axis=0, tiled=True),
        preferred_element_type=jnp.float32,
    )
    gate_pre = jnp.dot(
        normed,
        lax.all_gather(w_gate, "seq", axis=0, tiled=True),
        preferred_element_type=jnp.float32,
    )
    state = jnp.zeros((tok_rows, channels), jnp.float32)
    carried = jnp.zeros((channels,), jnp.float32)
    ones_row = jnp.ones((channels,), jnp.float32)
    for newton_step in range(NEWTON):
        previous = jnp.concatenate([carried[None, :], state[:-1]], axis=0)
        value, slope = cell(previous, cand_pre, gate_pre, rec_gate, rec_cand, bias_gate)
        offset = value - slope * previous
        sweep_a, sweep_b = lax.associative_scan(compose, (slope, offset), axis=0)
        entering = prefix((sweep_a[-1], sweep_b[-1]), "seq", compose, (ones_row, carried * 0.0))
        carried = entering[1]
        state = sweep_a * carried + sweep_b
    state_b = state.astype(jnp.bfloat16)
    partial_sums = jnp.dot(state_b, w_out, preferred_element_type=jnp.float32)
    summed = lax.psum_scatter(partial_sums, "mp", scatter_dimension=1, tiled=True)
    return summed.astype(jnp.bfloat16)


def solution(mesh):
    placed = (
        P("seq", "mp"),
        P(),
        P("seq", "mp"),
        P("seq", "mp"),
        P("mp"),
        P("mp"),
        P("mp"),
        P("mp", None),
    )
    return jax.shard_map(
        per_device, mesh=mesh, in_specs=placed, out_specs=P("seq", "mp"), check_vma=False
    )
```

profile of v0, /device:TPU:0, one launch (start us, length us, event | category | flops | bytes accessed | tf_op | source)
XLA Modules:
  0.0 296.8 jit_solution(11191967048189579970)
XLA Ops:
  8.8 30.8 %all-gather.10.cloned.1.call-done = bf16[128,4096]{1,0:T(8,128)(2,1)} async-done(((bf16[128,1024]{1,0:T(8,128)(2,1)}), bf16[128,4096]{1,0:T(8,128)(2,1)}) %all-gather.10.cloned.1.call-update) | async-done | bytes 1048592 | tf_op jit(solution)/shard_map/all_gather | solution.py:42
  39.6 1.5 fusion
  41.2 54.0 %all-gather.12.cloned.1.call-done = bf16[4096,1024]{1,0:T(8,128)(2,1)} async-done(((bf16[512,1024]{1,0:T(8,128)(2,1)}), bf16[4096,1024]{1,0:T(8,128)(2,1)}) %all-gather.12.cloned.1.call-update) | async-done | bytes 8388624 | tf_op jit(solution)/shard_map/all_gather | solution.py:53
  95.2 5.0 %fusion.26 = f32[128,1024]{1,0:T(8,128)S(1)} fusion(bf16[4096,1024]{1,0:T(8,128)(2,1)} %all-gather.12.cloned.1.call-done, bf16[128,4096]{1,0:T(8,128)(2,1)} %all-gather.10.cloned.1.call-done, f32[4096]{0:T(1024)S(1)} %copy-done.5, f32[128]{0:T(128)S(1)} %add_rsqrt_fusion), kind=kOutput, calls=%fused_computation.56 | convolution fusion | flops 1075838976 | bytes 9978368 | tf_op jit(solution)/shard_map/dot_general | solution.py:51
  100.2 51.2 %all-gather.14.cloned.1.call-done = bf16[4096,1024]{1,0:T(8,128)(2,1)} async-done(((bf16[512,1024]{1,0:T(8,128)(2,1)}), bf16[4096,1024]{1,0:T(8,128)(2,1)}) %all-gather.14.cloned.1.call-update) | async-done | bytes 8388624 | tf_op jit(solution)/shard_map/all_gather | solution.py:48
  151.4 5.1 %fusion.6 = (f32[128,1024]{1,0:T(8,128)S(1)}, f32[128,1024]{1,0:T(8,128)S(1)}, f32[128,1024]{1,0:T(8,128)S(1)}) fusion(f32[1024]{0:T(1024)S(1)} %copy-done.6, f32[1024]{0:T(1024)S(1)} %get-tuple-element.441, f32[1024]{0:T(1024)S(1)} %copy-done.7, f32[1024]{0:T(1024)S(1)} %copy-done.8, f32[128,1024]{1,0:T(8,128)S(1)} %fusion.26, ...), kind=kOutput, calls=%fused_computation.26 | convolution fusion | flops 1078722560 | bytes 11571712 | tf_op jit(solution)/shard_map/dot_general | solution.py:46
  156.9 0.8 slice.660
  157.7 1.0 fusion.59
  162.2 0.8 add_multiply_fusion.5
  163.1 1.7 pad.271
  164.9 1.7 pad.285
  167.5 9.1 %all-gather.1 = f32[8,1,1024]{2,1,0:T(1,128)S(1)} all-gather(f32[1,1,1024]{2,1,0:T(1,128)S(1)} %add_bitcast_fusion.4), channel_id=1, replica_groups=mesh['seq'=8,'mp'=4] {'seq'}, dimensions={0}, use_global_device_ids=true | all-gather | bytes 36864 | tf_op jit(solution)/shard_map/all_gather | solution.py:11
  177.4 8.2 %all-gather = f32[8,1,1024]{2,1,0:T(1,128)S(1)} all-gather(f32[1,1,1024]{2,1,0:T(1,128)S(1)} %add_bitcast_fusion.5), channel_id=1, replica_groups=mesh['seq'=8,'mp'=4] {'seq'}, dimensions={0}, use_global_device_ids=true | all-gather | bytes 36864 | tf_op jit(solution)/shard_map/all_gather | solution.py:11
  187.9 1.0 fusion.58
  192.5 0.8 add_multiply_fusion.3
  193.3 1.7 pad.299
  195.1 1.7 pad.313
  197.7 9.2 %all-gather.3 = f32[8,1,1024]{2,1,0:T(1,128)S(1)} all-gather(f32[1,1,1024]{2,1,0:T(1,128)S(1)} %add_bitcast_fusion.2), channel_id=1, replica_groups=mesh['seq'=8,'mp'=4] {'seq'}, dimensions={0}, use_global_device_ids=true | all-gather | bytes 36864 | tf_op jit(solution)/shard_map/all_gather | solution.py:11
  207.8 8.2 %all-gather.2 = f32[8,1,1024]{2,1,0:T(1,128)S(1)} all-gather(f32[1,1,1024]{2,1,0:T(1,128)S(1)} %add_bitcast_fusion.3), channel_id=1, replica_groups=mesh['seq'=8,'mp'=4] {'seq'}, dimensions={0}, use_global_device_ids=true | all-gather | bytes 36864 | tf_op jit(solution)/shard_map/all_gather | solution.py:11
  220.9 9.1 %all-gather.5 = f32[8,1,1024]{2,1,0:T(1,128)S(1)} all-gather(f32[1,1,1024]{2,1,0:T(1,128)S(1)} %add_bitcast_fusion), channel_id=1, replica_groups=mesh['seq'=8,'mp'=4] {'seq'}, dimensions={0}, use_global_device_ids=true | all-gather | bytes 36864 | tf_op jit(solution)/shard_map/all_gather | solution.py:11
  230.1 8.2 %all-gather.4 = f32[8,1,1024]{2,1,0:T(1,128)S(1)} all-gather(f32[1,1,1024]{2,1,0:T(1,128)S(1)} %add_bitcast_fusion.1), channel_id=1, replica_groups=mesh['seq'=8,'mp'=4] {'seq'}, dimensions={0}, use_global_device_ids=true | all-gather | bytes 36864 | tf_op jit(solution)/shard_map/all_gather | solution.py:11
  238.7 6.1 %fusion.28 = f32[128,4096]{1,0:T(8,128)} fusion(bf16[1024,4096]{1,0:T(8,128)(2,1)} %param.21, f32[128,1024]{1,0:T(8,128)S(1)} %pad.341, f32[128,1024]{1,0:T(8,128)S(1)} %pad.342, f32[128,1024]{1,0:T(8,128)S(1)} %pad.327, f32[128,1024]{1,0:T(8,128)S(1)} %pad.328, f32[1024]{0:T(1024)S(1)} %get-tuple-element.289), kind=kOutput, calls=%fused_computation.57 | convolution fusion | flops 1074397184 | bytes 12587008 | tf_op jit(solution)/shard_map/dot_general | solution.py:68
  244.8 43.8 %reduce-scatter.2.cloned.1.call-done = f32[128,1024]{1,0:T(8,128)} async-done(((f32[128,4096]{1,0:T(8,128)}), f32[128,1024]{1,0:T(8,128)}) %reduce-scatter.2.cloned.1.call-update) | async-done | bytes 524304 | tf_op jit(solution)/shard_map/reduce_scatter | solution.py:69
  288.5 1.8 convert_element_type.15
  (402 shorter events, 19.9 us)
Async XLA Ops:
  6.5 2.3 copy-start.7
  6.5 2.3 copy-start.6
  6.5 88.7 %copy-start.5 = (f32[4096]{0:T(1024)S(1)}, f32[4096]{0:T(1024)}, u32[]{:S(2)}) copy-start(f32[4096]{0:T(1024)} %param.15) | copy-start | bytes 49156
  6.5 33.1 %all-gather.10.cloned.1.call-start = ((), (), s32[]{:S(2)}) async-start(), calls=%async_computation.1 | async-start | bytes 1310720 | tf_op jit(solution)/shard_map/all_gather | solution.py:42
  7.3 87.9 %all-gather.12.cloned.1.call-start = ((), (), s32[]{:S(2)}) async-start(), calls=%async_computation.2 | async-start | bytes 9437184 | tf_op jit(solution)/shard_map/all_gather | solution.py:53
  8.0 143.4 %all-gather.14.cloned.1.call-start = ((), (), s32[]{:S(2)}) async-start(), calls=%async_computation.3 | async-start | bytes 9437184 | tf_op jit(solution)/shard_map/all_gather | solution.py:48
  8.7 279.8 %reduce-scatter.2.cloned.1.call-start = ((), (), s32[]{:S(2)}) async-start(), calls=%async_computation.4 | async-start | bytes 2621440 | tf_op jit(solution)/shard_map/reduce_scatter | solution.py:69
  41.2 110.2 %copy-start = (bf16[128,4096]{1,0:T(8,128)(2,1)S(1)}, bf16[128,4096]{1,0:T(8,128)(2,1)}, u32[]{:S(2)}) copy-start(bf16[128,4096]{1,0:T(8,128)(2,1)} %all-gather.10.cloned.1.call-done) | copy-start | bytes 3145732
  41.2 110.2 %copy-start.8 = (f32[1024]{0:T(1024)S(1)}, f32[1024]{0:T(1024)}, u32[]{:S(2)}) copy-start(f32[1024]{0:T(1024)} %param.20) | copy-start | bytes 12292
  163.0 1.8 copy-start.3
  163.0 3.6 %copy-start.1 = (f32[64,1024]{1,0:T(8,128)S(1)}, f32[64,1024]{1,0:T(8,128)}, u32[]{:S(2)}) copy-start(f32[64,1024]{1,0:T(8,128)} %add.628) | copy-start | bytes 786436
  193.3 1.8 copy-start.4
  193.3 3.6 %copy-start.2 = (f32[64,1024]{1,0:T(8,128)S(1)}, f32[64,1024]{1,0:T(8,128)}, u32[]{:S(2)}) copy-start(f32[64,1024]{1,0:T(8,128)} %add.663) | copy-start | bytes 786436
Sparse Core Ops, SparseCore 0:
  8.9 30.6 all-gather.9
  41.5 53.6 all-gather.11
  97.1 54.2 all-gather.13
  244.9 43.6 reduce-scatter.1
where the time goes:
time: 298 us; the launch traced here: 297 us
  waiting for transfers between devices  182 us (61%)
  blocking collectives  51.9 us (17%)
  local copies, waits for them, and re-layouts  16.1 us (5%)
  matrix products  16.1 us (5%)
  between operations  15.1 us (5%)
  other arithmetic  15 us (5%)
    all_gather x1, waiting for transfers between devices, per_device(): lax.all_gather(w_gate, 'seq', axis=0, tiled=True)  54 us
    all_gather x6, blocking collectives, prefix(): pieces = jax.tree.map(lambda part: lax.all_gather(part, axis), value)  51.9 us
    all_gather x1, waiting for transfers between devices, per_device(): lax.all_gather(w_cand, 'seq', axis=0, tiled=True)  51.2 us
    reduce_scatter x1, waiting for transfers between devices, per_device(): lax.psum_scatter(partial_sums, 'mp', scatter_dimension=1, tiled=True)  43.8 us
    all_gather x1, waiting for transfers between devices, per_device(): whole = lax.all_gather(tokens, 'mp', axis=1, tiled=True)  30.8 us
    pad x68, local copies, waits for them, and re-layouts, per_device(): sweep_a, sweep_b = lax.associative_scan(compose, (slope, offset), axis=0)  8.35 us
    slice x132, local copies, waits for them, and re-layouts, per_device(): sweep_a, sweep_b = lax.associative_scan(compose, (slope, offset), axis=0)  6.86 us
    dot_general x1, matrix products, per_device(): partial_sums = jnp.dot(state_b, w_out, preferred_element_type=jnp.float32)  6.06 us
  transfers between devices with their start and end apart: 4, of which 4 were waited for; matrix products, arithmetic and copies ran while one was open for 2% of the time, Pallas kernels for 0%

commit v1 on v0

--- a/solution.py
+++ b/solution.py
@@ -4,6 +4,18 @@
 from jax.sharding import PartitionSpec as P
 
 NEWTON = 3
+
+
+def collect(x, axis, dim):
+    ways, here, step = (lax.axis_size(axis), lax.axis_index(axis), x.shape[dim])
+    line, have = (x, 1)
+    while have < ways:
+        line = jnp.concatenate(
+            [line, lax.ppermute(line, axis, [(d, (d - have) % ways) for d in range(ways)])],
+            axis=dim,
+        )
+        have = 2 * have
+    return jnp.roll(line, here * step, axis=dim)
 
 
 def prefix(value, axis, join, neutral):
@@ -43,11 +55,7 @@
     wide = whole.astype(jnp.float32)
     factor = lax.rsqrt(jnp.mean(wide * wide, axis=1, keepdims=True) + 1e-05)
     normed = (wide * factor * norm_gain).astype(jnp.bfloat16)
-    cand_pre = jnp.dot(
-        normed,
-        lax.all_gather(w_cand, "seq", axis=0, tiled=True),
-        preferred_element_type=jnp.float32,
-    )
+    cand_pre = jnp.dot(normed, collect(w_cand, "seq", 0), preferred_element_type=jnp.float32)
     gate_pre = jnp.dot(
         normed,
         lax.all_gather(w_gate, "seq", axis=0, tiled=True),

time: 298 us -> 367 us (1.23)
  waiting for transfers between devices: 182 us -> 225 us
  local copies, waits for them, and re-layouts: 16.1 us -> 33.8 us
  other arithmetic: 15 us -> 19.3 us
  starting transfers between devices: 0.12 us -> 4.12 us
    ppermute x0 -> x3, waiting for transfers between devices: none -> 180 us  [collect(): lax.ppermute(line, axis, [(d, (d - have) % ways) for d in range(ways)])]
    all_gather x1, waiting for transfers between devices: 54 us -> 0.01 us  [per_device(): lax.all_gather(w_gate, 'seq', axis=0, tiled=True)]
    all_gather x1 -> x0, waiting for transfers between devices: 51.2 us -> none  [per_device(): lax.all_gather(w_cand, 'seq', axis=0, tiled=True)]
    all_gather x1, waiting for transfers between devices: 30.8 us -> 0.01 us  [per_device(): whole = lax.all_gather(tokens, 'mp', axis=1, tiled=True)]
    unnamed x28 -> x37, local copies, waits for them, and re-layouts: 0.36 us -> 15.5 us
    concatenate x0 -> x2, other arithmetic: none -> 5.22 us  [collect(): jnp.concatenate([line, lax.ppermute(line, axis, [(d, (d - have) % ways) f...]
    concatenate x0 -> x1, local copies, waits for them, and re-layouts: none -> 4.56 us  [collect(): return jnp.roll(line, here * step, axis=dim)]
    ppermute x0 -> x3, starting transfers between devices: none -> 4.04 us  [collect(): lax.ppermute(line, axis, [(d, (d - have) % ways) for d in range(ways)])]
  transfers between devices with their start and end apart: 4 -> 6, of which waited for: 4 -> 4; matrix products, arithmetic and copies ran while one was open for 2% -> 7% of each run, Pallas kernels for 0% -> 0%
where the time goes in v1:
time: 367 us; the launch traced here: 366 us
  waiting for transfers between devices  225 us (61%)
  blocking collectives  51.9 us (14%)
  local copies, waits for them, and re-layouts  33.8 us (9%)
  other arithmetic  19.3 us (5%)
  matrix products  15.8 us (4%)
  between operations  15.1 us (4%)
  starting transfers between devices  4.12 us (1%)
    ppermute x3, waiting for transfers between devices, collect(): lax.ppermute(line, axis, [(d, (d - have) % ways) for d in range(ways)])  180 us
    all_gather x6, blocking collectives, prefix(): pieces = jax.tree.map(lambda part: lax.all_gather(part, axis), value)  51.9 us
    reduce_scatter x1, waiting for transfers between devices, per_device(): lax.psum_scatter(partial_sums, 'mp', scatter_dimension=1, tiled=True)  44.1 us
    unnamed x37, local copies, waits for them, and re-layouts  15.5 us
    slice x132, local copies, waits for them, and re-layouts, per_device(): sweep_a, sweep_b = lax.associative_scan(compose, (slope, offset), axis=0)  8.1 us
  transfers between devices with their start and end apart: 6, of which 4 were waited for; matrix products, arithmetic and copies ran while one was open for 7% of the time, Pallas kernels for 0%

profile of v1, /device:TPU:0, one launch (start us, length us, event | category | flops | bytes accessed | tf_op | source)
XLA Modules:
  0.0 366.1 jit_solution(637851280416524105)
XLA Ops:
  8.1 3.4 collective-permute-start
  11.5 12.6 %collective-permute-done = bf16[512,1024]{1,0:T(8,128)(2,1)S(1)} collective-permute-done((bf16[512,1024]{1,0:T(8,128)(2,1)}, bf16[512,1024]{1,0:T(8,128)(2,1)S(1)}, u32[]{:S(2)}, u32[]{:S(2)}) %collective-permute-start) | collective-permute-done | bytes 1048608 | tf_op jit(solution)/shard_map/ppermute | solution.py:14
  24.1 1.9 pad_maximum_fusion.1
  26.6 59.0 %collective-permute-done.1 = bf16[1024,1024]{1,0:T(8,128)(2,1)S(1)} collective-permute-done((bf16[1024,1024]{1,0:T(8,128)(2,1)S(1)}, bf16[1024,1024]{1,0:T(8,128)(2,1)S(1)}, u32[]{:S(2)}, u32[]{:S(2)}) %collective-permute-start.1) | collective-permute-done | bytes 2097184 | tf_op jit(solution)/shard_map/ppermute | solution.py:14
  85.6 3.4 pad_maximum_fusion
  90.1 2.3 constant_dynamic-update-slice_fusion.6
  92.4 1.9 fusion.2
  95.8 108.3 %collective-permute-done.2 = bf16[2048,1024]{1,0:T(8,128)(2,1)} collective-permute-done((bf16[2048,1024]{1,0:T(8,128)(2,1)}, bf16[2048,1024]{1,0:T(8,128)(2,1)}, u32[]{:S(2)}, u32[]{:S(2)}) %collective-permute-start.2) | collective-permute-done | bytes 4194336 | tf_op jit(solution)/shard_map/ppermute | solution.py:14
  204.2 4.6 %constant_dynamic-update-slice_fusion.4 = bf16[8192,1024]{1,0:T(8,128)(2,1)} fusion(bf16[8192,1024]{1,0:T(8,128)(2,1)} %constant_dynamic-update-slice_fusion.5, bf16[2048,1024]{1,0:T(8,128)(2,1)} %collective-permute-done.2), kind=kLoop, calls=%fused_computation.144 | loop fusion | bytes 8388608
  210.9 1.6 constant_dynamic-update-slice_fusion.1
  212.5 4.6 %constant_dynamic-update-slice_fusion = bf16[8192,1024]{1,0:T(8,128)(2,1)} fusion(bf16[8192,1024]{1,0:T(8,128)(2,1)} %constant_dynamic-update-slice_fusion.1, bf16[2048,1024]{1,0:T(8,128)(2,1)} %collective-permute-done.2), kind=kLoop, calls=%fused_computation.140 | loop fusion | bytes 8388608 | tf_op jit(solution)/shard_map/jit(_roll_dynamic)/concatenate | solution.py:18
  217.0 4.7 %fusion.27 = f32[128,1024]{1,0:T(8,128)S(1)} fusion(bf16[4096,1024]{1,0:T(8,128)(2,1)} %all-gather.11.cloned.1.call-done, bf16[128,4096]{1,0:T(8,128)(2,1)S(1)} %copy-done.3, f32[4096]{0:T(1024)S(1)} %copy-done.6, f32[128]{0:T(128)S(1)} %add_rsqrt_fusion), kind=kOutput, calls=%fused_computation.59 | convolution fusion | flops 1075838976 | bytes 9978368 | tf_op jit(solution)/shard_map/dot_general | solution.py:59
  221.7 5.1 %fusion.8 = (f32[128,1024]{1,0:T(8,128)S(1)}, f32[128,1024]{1,0:T(8,128)S(1)}, f32[128,1024]{1,0:T(8,128)S(1)}) fusion(f32[1024]{0:T(1024)S(1)} %copy-done.7, f32[1024]{0:T(1024)S(1)} %get-tuple-element.441, f32[1024]{0:T(1024)S(1)} %copy-done.8, f32[1024]{0:T(1024)S(1)} %copy-done.9, f32[128,1024]{1,0:T(8,128)S(1)} %fusion.27, ...), kind=kOutput, calls=%fused_computation.30 | convolution fusion | flops 1078722560 | bytes 11571716 | tf_op jit(solution)/shard_map/dot_general | solution.py:58
  234.6 1.7 pad.271
  238.6 8.2 %all-gather.1 = f32[8,1,1024]{2,1,0:T(1,128)S(1)} all-gather(f32[1,1,1024]{2,1,0:T(1,128)S(1)} %add_bitcast_fusion.4), channel_id=1, replica_groups=mesh['seq'=8,'mp'=4] {'seq'}, dimensions={0}, use_global_device_ids=true | all-gather | bytes 36864 | tf_op jit(solution)/shard_map/all_gather | solution.py:23
  247.6 9.3 %all-gather = f32[8,1,1024]{2,1,0:T(1,128)S(1)} all-gather(f32[1,1,1024]{2,1,0:T(1,128)S(1)} %add_bitcast_fusion.5), channel_id=1, replica_groups=mesh['seq'=8,'mp'=4] {'seq'}, dimensions={0}, use_global_device_ids=true | all-gather | bytes 36864 | tf_op jit(solution)/shard_map/all_gather | solution.py:23
  263.9 1.7 pad.299
  266.9 8.2 %all-gather.3 = f32[8,1,1024]{2,1,0:T(1,128)S(1)} all-gather(f32[1,1,1024]{2,1,0:T(1,128)S(1)} %add_bitcast_fusion.2), channel_id=1, replica_groups=mesh['seq'=8,'mp'=4] {'seq'}, dimensions={0}, use_global_device_ids=true | all-gather | bytes 36864 | tf_op jit(solution)/shard_map/all_gather | solution.py:23
  275.9 9.1 %all-gather.2 = f32[8,1,1024]{2,1,0:T(1,128)S(1)} all-gather(f32[1,1,1024]{2,1,0:T(1,128)S(1)} %add_bitcast_fusion.3), channel_id=1, replica_groups=mesh['seq'=8,'mp'=4] {'seq'}, dimensions={0}, use_global_device_ids=true | all-gather | bytes 36864 | tf_op jit(solution)/shard_map/all_gather | solution.py:23
  289.8 8.2 %all-gather.5 = f32[8,1,1024]{2,1,0:T(1,128)S(1)} all-gather(f32[1,1,1024]{2,1,0:T(1,128)S(1)} %add_bitcast_fusion), channel_id=1, replica_groups=mesh['seq'=8,'mp'=4] {'seq'}, dimensions={0}, use_global_device_ids=true | all-gather | bytes 36864 | tf_op jit(solution)/shard_map/all_gather | solution.py:23
  298.2 9.1 %all-gather.4 = f32[8,1,1024]{2,1,0:T(1,128)S(1)} all-gather(f32[1,1,1024]{2,1,0:T(1,128)S(1)} %add_bitcast_fusion.1), channel_id=1, replica_groups=mesh['seq'=8,'mp'=4] {'seq'}, dimensions={0}, use_global_device_ids=true | all-gather | bytes 36864 | tf_op jit(solution)/shard_map/all_gather | solution.py:23
  307.6 6.1 %fusion.29 = f32[128,4096]{1,0:T(8,128)} fusion(bf16[1024,4096]{1,0:T(8,128)(2,1)} %param.21, f32[128,1024]{1,0:T(8,128)S(1)} %pad.341, f32[128,1024]{1,0:T(8,128)S(1)} %pad.342, f32[128,1024]{1,0:T(8,128)S(1)} %pad.327, f32[128,1024]{1,0:T(8,128)S(1)} %pad.328, f32[1024]{0:T(1024)S(1)} %get-tuple-element.289), kind=kOutput, calls=%fused_computation.60 | convolution fusion | flops 1074397184 | bytes 12587008 | tf_op jit(solution)/shard_map/dot_general | solution.py:76
  313.7 44.1 %reduce-scatter.2.cloned.1.call-done = f32[128,1024]{1,0:T(8,128)} async-done(((f32[128,4096]{1,0:T(8,128)}), f32[128,1024]{1,0:T(8,128)}) %reduce-scatter.2.cloned.1.call-update) | async-done | bytes 524304 | tf_op jit(solution)/shard_map/reduce_scatter | solution.py:77
  357.8 1.8 convert_element_type.15
  (417 shorter events, 30.9 us)
Async XLA Ops:
  6.5 82.4 %copy-start = (bf16[512,1024]{1,0:T(8,128)(2,1)S(1)}, bf16[512,1024]{1,0:T(8,128)(2,1)}, u32[]{:S(2)}) copy-start(bf16[512,1024]{1,0:T(8,128)(2,1)} %param.16) | copy-start | bytes 3145732
  6.5 83.5 %copy-start.8 = (f32[1024]{0:T(1024)S(1)}, f32[1024]{0:T(1024)}, u32[]{:S(2)}) copy-start(f32[1024]{0:T(1024)} %param.18) | copy-start | bytes 12292
  6.5 83.5 %copy-start.7 = (f32[1024]{0:T(1024)S(1)}, f32[1024]{0:T(1024)}, u32[]{:S(2)}) copy-start(f32[1024]{0:T(1024)} %param.19) | copy-start | bytes 12292
  6.5 85.8 %all-gather.9.cloned.1.call-start = ((), (), s32[]{:S(2)}) async-start(), calls=%async_computation.1 | async-start | bytes 1310720 | tf_op jit(solution)/shard_map/all_gather | solution.py:54
  7.3 209.8 %all-gather.11.cloned.1.call-start = ((), (), s32[]{:S(2)}) async-start(), calls=%async_computation.2 | async-start | bytes 9437184 | tf_op jit(solution)/shard_map/all_gather | solution.py:61
  8.0 349.8 %reduce-scatter.2.cloned.1.call-start = ((), (), s32[]{:S(2)}) async-start(), calls=%async_computation.3 | async-start | bytes 2621440 | tf_op jit(solution)/shard_map/reduce_scatter | solution.py:77
  8.1 16.0 %collective-permute-start = (bf16[512,1024]{1,0:T(8,128)(2,1)}, bf16[512,1024]{1,0:T(8,128)(2,1)S(1)}, u32[]{:S(2)}, u32[]{:S(2)}) collective-permute-start(bf16[512,1024]{1,0:T(8,128)(2,1)} %param.16), channel_id=1, source_target_pairs={{0,28},{4,0},{8,4},{12,8},{16,12},{20,16},{24,20},{28,24},{1,29},{... | collective-permute-start | bytes 3145736 | tf_op jit(solution)/shard_map/ppermute | solution.py:14
  24.1 61.5 %copy-start.1 = (bf16[512,1024]{1,0:T(8,128)(2,1)}, bf16[512,1024]{1,0:T(8,128)(2,1)S(1)}, u32[]{:S(2)}) copy-start(bf16[512,1024]{1,0:T(8,128)(2,1)S(1)} %collective-permute-done) | copy-start | bytes 3145732
  26.0 59.6 %collective-permute-start.1 = (bf16[1024,1024]{1,0:T(8,128)(2,1)S(1)}, bf16[1024,1024]{1,0:T(8,128)(2,1)S(1)}, u32[]{:S(2)}, u32[]{:S(2)}) collective-permute-start(bf16[1024,1024]{1,0:T(8,128)(2,1)S(1)} %pad_maximum_fusion.1), channel_id=1, source_target_pairs={{0,24},{4,28},{8,0},{12,4},{16,8},{20,12},{24,16},{28,20},{1,25},{... | collective-permute-start | bytes 6291464 | tf_op jit(solution)/shard_map/ppermute | solution.py:14
  89.0 115.2 %collective-permute-start.2 = (bf16[2048,1024]{1,0:T(8,128)(2,1)}, bf16[2048,1024]{1,0:T(8,128)(2,1)}, u32[]{:S(2)}, u32[]{:S(2)}) collective-permute-start(bf16[2048,1024]{1,0:T(8,128)(2,1)} %pad_maximum_fusion), channel_id=1, source_target_pairs={{0,16},{4,20},{8,24},{12,28},{16,0},{20,4},{24,8},{28,12},{1,17},{... | collective-permute-start | bytes 12582920 | tf_op jit(solution)/shard_map/ppermute | solution.py:14
  92.4 117.5 %copy-start.2 = (bf16[512,1024]{1,0:T(8,128)(2,1)S(1)}, bf16[512,1024]{1,0:T(8,128)(2,1)}, u32[]{:S(2)}) copy-start(bf16[512,1024]{1,0:T(8,128)(2,1)} %copy-done.1) | copy-start | bytes 3145732
  208.8 8.2 %copy-start.6 = (f32[4096]{0:T(1024)S(1)}, f32[4096]{0:T(1024)}, u32[]{:S(2)}) copy-start(f32[4096]{0:T(1024)} %param.15) | copy-start | bytes 49156
  209.8 7.2 %copy-start.3 = (bf16[128,4096]{1,0:T(8,128)(2,1)S(1)}, bf16[128,4096]{1,0:T(8,128)(2,1)}, u32[]{:S(2)}) copy-start(bf16[128,4096]{1,0:T(8,128)(2,1)} %all-gather.9.cloned.1.call-done) | copy-start | bytes 3145732
  217.0 4.7 %copy-start.9 = (f32[1024]{0:T(1024)S(1)}, f32[1024]{0:T(1024)}, u32[]{:S(2)}) copy-start(f32[1024]{0:T(1024)} %param.20) | copy-start | bytes 12292
  232.0 1.8 copy-start.4
  232.0 1.8 copy-start.5
Sparse Core Ops, SparseCore 0:
  8.9 30.6 all-gather.8
  41.5 99.3 all-gather.10
  313.8 43.9 reduce-scatter.1
